TPU v7x, 32 devices: a whole 2x2x4 slice. The times are simulated.
32 devices in a mesh: run: 2 (over y), team: 4 (over x, core), ma: 4 (over z).
Axes of the slice: x: 2, y: 2, z: 4, core: 2. Of those that a mesh axis runs over, the one named last changes fastest.
Arguments:
- section: bfloat16 [8, 2, 3, 24, 2, 32896], P(('run', 'team'), None, None, None, None, 'ma'), parts along dimension 0, may hold values from -6 to 6
- start: float32 [8, 2, 3, 24, 2, 32896], P(('run', 'team'), None, None, None, None, 'ma'), parts along dimension 0, may hold values from -6 to 6
- velocity: bfloat16 [768, 3, 24, 768], P(('run', 'ma'), None, 'team'), parts along dimension 0, may hold values from -6 to 6
- pair_list: int32 [128], P('ma'), may hold values from 0 to 127, each once
- wavenumber: int32 [4], P('team'), may hold values from 1 to 23
Outputs:
- updated: float32 [8, 2, 3, 24, 2, 32896], P(('run', 'team'), None, None, None, None, 'ma'), parts along dimension 0
There are 2 independent parts, one for each index of `run`. A program takes and returns all parts, laid end to end along the dimension named above; an argument that names none is the same for every part. Nothing has to cross between parts.
Inputs may be any that keep to these rules, and one draw needn't show every extreme that they name: Block q of the rows holds orders pair_list[q] and 255 - pair_list[q]; each value appears once.
All inputs are finite; a program needn't handle non-finite values.
Results may differ from a plain program's by a relative error of at most 0.0078.
Values may be sent and summed in bfloat16 or wider, within the bound.
No kernel may reach another device: no remote copies, remote signals or barrier semaphores. Data moves between devices by JAX's collectives and lax.ppermute only.
A program may use at most 320 MiB of HBM per device.

v0:
```python
import math

import jax
import jax.numpy as jnp
from jax import lax
from jax.sharding import PartitionSpec as P

NM = 256
NLAT = 384
NLON = 768
LEV = 24
TESTS = 2


grid_scale = 1.0 / 64.0
anchor_gain = 64.0 * math.sqrt(4.0 * math.pi)
quadrature_gain = 64.0
diffusion = 7e-06
step_weight = 2.0
row_block = 16


def seed_values(order_real, order_count, sine_theta):
    factor_index = jnp.arange(1, order_count, dtype=jnp.float32)
    factor_log = jnp.log((2.0 * factor_index - 1.0) / (2.0 * factor_index))
    partial_log = jnp.sum(
        jnp.where(factor_index[None, :] <= order_real[:, None], factor_log[None, :], 0.0), axis=1
    )
    seed_log = 0.5 * (jnp.log((2.0 * order_real + 1.0) / (4.0 * jnp.pi)) + partial_log)
    return jnp.exp(seed_log[:, None] + order_real[:, None] * jnp.log(sine_theta)[None, :])


def pair_table(pair_ids, order_count, lat_count):
    pair_count = pair_ids.shape[0]
    order_low = pair_ids.astype(jnp.float32)
    order_high = (order_count - 1 - pair_ids).astype(jnp.float32)
    colatitude = jnp.pi * (jnp.arange(lat_count, dtype=jnp.float32) + 0.5) / lat_count
    cosine = jnp.cos(colatitude)
    sine_theta = jnp.sin(colatitude)
    seed_low = seed_values(order_low, order_count, sine_theta)
    seed_high = seed_values(order_high, order_count, sine_theta)
    switch_row = order_count - pair_ids

    def one_row(state_pair, row_id):
        latest, before = state_pair
        in_low = row_id < switch_row
        degree = jnp.where(in_low, pair_ids + row_id, row_id - 1)
        order_real = jnp.where(in_low, order_low, order_high)
        degree_real = degree.astype(jnp.float32)
        active = degree_real > order_real
        divisor = jnp.where(active, degree_real * degree_real - order_real * order_real, 1.0)
        upper = jnp.sqrt(jnp.maximum(4.0 * degree_real * degree_real - 1.0, 0.0) / divisor)
        lower_num = ((degree_real - 1.0) * (degree_real - 1.0) - order_real * order_real) * (
            2.0 * degree_real + 1.0
        )
        lower = jnp.sqrt(
            jnp.maximum(lower_num, 0.0) / (divisor * jnp.maximum(2.0 * degree_real - 3.0, 1.0))
        )
        recurred = upper[:, None] * cosine[None, :] * latest - lower[:, None] * before
        is_seed = (row_id == 0) | (row_id == switch_row)
        seeded = jnp.where(in_low[:, None], seed_low, seed_high)
        current = jnp.where(is_seed[:, None], seeded, jnp.where(active[:, None], recurred, 0.0))
        return ((current, latest), current)

    def block_rows(state_pair, first_row):
        produced = []
        for offset in range(row_block):
            state_pair, current = one_row(state_pair, first_row + offset)
            produced.append(current)
        return (state_pair, jnp.stack(produced))

    turns = -(-(order_count + 1) // row_block)
    blank_rows = jnp.zeros((pair_count, lat_count), jnp.float32)
    firsts = jnp.arange(turns, dtype=jnp.int32) * row_block
    _, values = lax.scan(block_rows, (blank_rows, blank_rows), firsts)
    leg_table = values.reshape(turns * row_block, pair_count, lat_count)[: order_count + 1]
    row_index = jnp.arange(order_count + 1, dtype=jnp.int32)
    first_half = row_index[None, :] < (order_count - pair_ids)[:, None]
    degree = jnp.where(first_half, pair_ids[:, None] + row_index[None, :], row_index[None, :] - 1)
    return (leg_table, first_half, degree)


def wave_table(order_list, lon_count):
    longitude = jnp.arange(lon_count, dtype=jnp.int32)
    phase_index = order_list[:, None] * longitude[None, :] % lon_count
    angle_rad = 2.0 * jnp.pi / lon_count * phase_index.astype(jnp.float32)
    return jnp.stack([jnp.cos(angle_rad), jnp.sin(angle_rad)])


def lat_weights(latitudes, lat_count):
    colatitude = jnp.pi * (latitudes.astype(jnp.float32) + 0.5) / lat_count
    return quadrature_gain * (jnp.pi / lat_count) * jnp.sin(colatitude)


def test_field(wave_index, test_count, levels):
    component = jnp.arange(3, dtype=jnp.int32)
    test_ids = jnp.arange(test_count, dtype=jnp.int32)
    level_ids = jnp.arange(levels, dtype=jnp.float32)
    aligned = (component[None, :] == test_ids[:, None]).astype(jnp.float32)
    profile = jnp.cos(jnp.pi * wave_index.astype(jnp.float32) * (level_ids + 0.5) / levels)
    return anchor_gain * aligned[:, :, None] * profile[None, None, :]


def cross_field(motion, magnetic, along):
    return jnp.roll(motion, -1, along) * jnp.roll(magnetic, -2, along) - jnp.roll(
        motion, -2, along
    ) * jnp.roll(magnetic, -1, along)


def shards(section, start, velocity, pair_list, wavenumber):
    pair_count = pair_list.shape[0]
    leg_table, first_half, degree = pair_table(pair_list, NM, NLAT)
    legendre = leg_table.astype(jnp.bfloat16)
    selectors = jnp.stack([first_half, jnp.logical_not(first_half)], axis=1)
    masks_low = selectors.astype(jnp.bfloat16)
    anchor = (pair_list == 0)[:, None] & (jnp.arange(NM + 1) == 0)[None, :]
    anchor_rows = anchor.reshape(-1).astype(jnp.float32)
    part_pick = jnp.array([1.0, 0.0], jnp.float32)
    forcing = test_field(wavenumber[0], TESTS, LEV)
    spec_field = (
        section[0].astype(jnp.float32)
        + forcing[:, :, :, None, None] * part_pick[:, None] * anchor_rows[None, :]
    )
    spec_field = spec_field.astype(jnp.bfloat16).reshape(TESTS, 3, LEV, 2, pair_count, NM + 1)
    masked = spec_field[:, :, :, :, :, None, :] * masks_low
    spectra = jnp.einsum(
        "scvpqhr,rqa->ascvpqh", masked, legendre, preferred_element_type=jnp.float32
    )
    spectra = spectra.astype(jnp.bfloat16).reshape(NLAT, TESTS, 3, LEV, 2, 2 * pair_count)
    every_pair = lax.all_gather(pair_list, "ma", axis=0, tiled=True)
    order_list = jnp.stack([every_pair, NM - 1 - every_pair], axis=1).reshape(-1)
    waves = wave_table(order_list, NLON)
    inverse_table = (waves * grid_scale).astype(jnp.bfloat16)
    forward_table = (waves * (2.0 * jnp.pi / NLON)).astype(jnp.bfloat16)
    wind_field = lax.all_gather(velocity, "team", axis=2, tiled=True)
    band_size = velocity.shape[0]
    latitudes = lax.axis_index("ma") * band_size + jnp.arange(band_size, dtype=jnp.int32)
    weights = lat_weights(latitudes, NLAT)
    collected = []
    for test_id in range(TESTS):
        grid_field = jnp.einsum(
            "ascvpm,pmo->ascvo",
            lax.all_to_all(
                spectra[:, test_id : test_id + 1], "ma", split_axis=0, concat_axis=5, tiled=True
            ),
            inverse_table,
            preferred_element_type=jnp.float32,
        )
        emf = cross_field(wind_field[:, None], grid_field, 2).astype(jnp.bfloat16)
        fourier = jnp.einsum(
            "ascvo,pmo->ascvpm", emf, forward_table, preferred_element_type=jnp.float32
        )
        fourier = (fourier * weights[:, None, None, None, None, None]).astype(jnp.bfloat16)
        collected.append(lax.all_to_all(fourier, "ma", split_axis=5, concat_axis=0, tiled=True))
    returned = jnp.concatenate(collected, axis=1)
    returned = returned.reshape(NLAT, TESTS, 3, LEV, 2, pair_count, 2)
    project = jnp.einsum(
        "ascvpqh,rqa->scvpqhr", returned, legendre, preferred_element_type=jnp.float32
    )
    tendency = jnp.sum(project * selectors.astype(jnp.float32), axis=5).reshape(
        TESTS, 3, LEV, 2, -1
    )
    spread = (degree * (degree + 1)).astype(jnp.float32).reshape(-1)
    updated = start[0] + step_weight * (
        tendency - diffusion * spread * section[0].astype(jnp.float32)
    )
    return updated[None]


def solution(mesh):
    placed = (
        P(("run", "team"), None, None, None, None, "ma"),
        P(("run", "team"), None, None, None, None, "ma"),
        P(("run", "ma"), None, "team", None),
        P("ma"),
        P("team"),
    )
    return jax.shard_map(
        shards,
        mesh=mesh,
        in_specs=placed,
        out_specs=P(("run", "team"), None, None, None, None, "ma"),
        check_vma=False,
    )
```

profile of v0, /device:TPU:0, one launch (start us, length us, event | category | flops | bytes accessed | tf_op | source)
XLA Modules:
  0.0 1409.3 jit_solution(6783908820173392314)
XLA Ops:
  9.1 265.7 %while.23 = (s32[]{:T(128)}, f32[32,384]{1,0:T(8,128)S(1)}, f32[32,384]{1,0:T(8,128)S(1)}, bf16[17,16,32,384]{3,2,1,0:T(8,128)(2,1)}, s32[17]{0:T(128)S(1)}, /*i...) while((s32[]{:T(128)}, f32[32,384]{1,0:T(8,128)S(1)}, ...), condition=%wide.region_3.4_spmd.clone.clone.clone.clone, body=%wide.region_2.3_spmd.clone.clone.clone.clone.sunk | while | flops 2215714 | bytes 4084432 | solution.py:75
  287.5 17.2 %reshape.1598 = f32[2,3,24,2,32,257]{5,4,2,3,1,0:T(8,128)} reshape(f32[1,2,3,24,2,8224]{5,3,4,2,1,0:T(8,128)} %copy_convert_fusion) | data formatting | bytes 18948096 | tf_op jit(solution)/shard_map/convert_element_type | solution.py:121
  324.3 25.8 %convert_bitcast_fusion = bf16[384,2,3,24,2,32,2]{0,3,6,4,2,1,5:T(8,128)(2,1)} fusion(bf16[32,2,257]{2,1,0:T(2,128)(2,1)S(1)} %get-tuple-element.835, bf16[2,3,24,2,32,257]{5,2,3,1,0,4:T(8,128)(2,1)} %copy.141, bf16[272,32,384]{2,0,1:T(8,128)(2,1)} %bitcast.212), kind=kOutput, calls=%fused_computation.270 | convolution fusion | flops 3664060416 | bytes 27754624 | tf_op jit(solution)/shard_map/scvpqhr,rqa->ascvpqh/dot_general | solution.py:126
  362.4 17.9 %copy.143 = bf16[384,1,3,24,2,64]{5,3,4,2,1,0:T(8,128)(2,1)} copy(bf16[384,1,3,24,2,64]{0,3,5,4,2,1:T(8,128)(2,1)} %get-tuple-element.829) | data formatting | bytes 14155776 | tf_op jit(solution)/shard_map/slice | solution.py:144
  380.3 14.2 %reshape.1613 = bf16[4,2,442368]{2,1,0:T(2,128)(2,1)} reshape(bf16[384,1,3,2,24,64]{5,4,3,2,1,0:T(8,128)(2,1)} %bitcast.200) | data formatting | bytes 14155776
  402.8 18.4 %copy.154 = bf16[384,1,3,24,2,64]{5,3,4,2,1,0:T(8,128)(2,1)} copy(bf16[384,1,3,24,2,64]{0,3,5,4,2,1:T(8,128)(2,1)} %get-tuple-element.830) | data formatting | bytes 14155776 | tf_op jit(solution)/shard_map/slice | solution.py:144
  421.2 14.3 %reshape.1611 = bf16[4,2,442368]{2,1,0:T(2,128)(2,1)} reshape(bf16[384,1,3,2,24,64]{5,4,3,2,1,0:T(8,128)(2,1)} %bitcast.201) | data formatting | bytes 14155776
  435.5 121.4 %all-to-all-done = bf16[4,2,442368]{2,1,0:T(2,128)(2,1)} async-done(((bf16[4,2,442368]{2,1,0:T(2,128)(2,1)}), bf16[4,2,442368]{2,1,0:T(2,128)(2,1)}, u32[]{:S(2)}, u32[]{:S(2)}) %all-to-all-start) | async-done | bytes 7077920 | tf_op jit(solution)/shard_map/all_to_all | solution.py:143
  563.8 153.3 %all-reduce = s32[128]{0:T(128)S(1)} all-reduce(s32[128]{0:T(128)S(1)} %dynamic-update-slice), channel_id=1, replica_groups=mesh['run'=2,'team'=4,'ma'=4] {'ma'}, use_global_device_ids=true, to_apply=%add | all-reduce | flops 128 | bytes 1024
  720.7 14.5 %reshape.1614 = bf16[384,1,3,2,24,64]{5,4,3,2,1,0:T(8,128)(2,1)} reshape(bf16[4,2,442368]{2,1,0:T(2,128)(2,1)} %all-to-all-done) | data formatting | bytes 14155776
  735.2 19.3 %copy.177 = bf16[4,96,1,3,24,2,64]{1,0,6,5,4,3,2:T(4,128)(2,1)} copy(bf16[4,96,1,3,24,2,64]{6,4,5,3,1,0,2:T(8,128)(2,1)} %bitcast.202) | data formatting | bytes 14155776 | tf_op jit(solution)/shard_map/all_to_all | solution.py:143
  776.6 14.9 %convolution_bitcast_fusion.1 = f32[96,1,3,24,768]{4,3,2,0,1:T(8,128)} fusion(bf16[96,3,24,2,256]{4,2,3,1,0:T(8,128)(2,1)} %copy.147, f32[1,256,768]{2,1,0:T(8,128)S(1)} %get-tuple-element.838, f32[1,256,768]{2,1,0:T(8,128)S(1)} %get-tuple-element.837), kind=kOutput, calls=%fused_computation.283 | convolution fusion | flops 5436997632 | bytes 29884416 | tf_op jit(solution)/shard_map/ascvpm,pmo->ascvo/dot_general | solution.py:141
  802.7 18.5 %slice_bitcast_fusion.3 = (f32[96,2,24,768]{3,2,1,0:T(8,128)}, f32[96,2,24,768]{3,2,1,0:T(8,128)}) fusion(f32[96,1,3,24,768]{4,3,2,0,1:T(8,128)} %convolution_bitcast_fusion.1), kind=kLoop, calls=%fused_computation.264 | loop fusion | bytes 56623104 | tf_op jit(solution)/shard_map/jit(_roll_static)/concatenate | solution.py:105
  838.0 23.3 %fusion.145 = bf16[96,1,3,24,2,256]{5,3,4,2,0,1:T(8,128)(2,1)} fusion(f32[96]{0:T(128)S(1)} %sine_multiply_fusion, f32[96,1,24,768]{3,2,1,0:T(8,128)} %get-tuple-element.822, f32[96,2,24,768]{3,2,1,0:T(8,128)} %get-tuple-element.824, f32[96,2,24,768]{3,2,1,0:T(8,128)} %get-tuple-element.823, f32[96,1,24,768]{3,2,1,0:T(8,128)} %get-tuple-element.821, ...), kind=kOutput, calls=%fused_computation.293 | convolution fusion | flops 5518393344 | bytes 72352128 | tf_op jit(solution)/shard_map/ascvo,pmo->ascvpm/dot_general | solution.py:150
  894.1 19.3 %copy.178 = bf16[4,96,1,3,24,2,64]{1,0,6,5,4,3,2:T(4,128)(2,1)} copy(bf16[4,96,1,3,24,2,64]{6,4,5,3,1,0,2:T(8,128)(2,1)} %bitcast.203) | data formatting | bytes 14155776 | tf_op jit(solution)/shard_map/all_to_all | solution.py:143
  959.2 19.0 %slice_bitcast_fusion.1 = (f32[96,2,24,768]{3,2,0,1:T(8,128)}, f32[96,2,24,768]{3,2,0,1:T(8,128)}) fusion(f32[96,1,3,24,768]{4,3,0,2,1:T(8,128)} %convolution_bitcast_fusion), kind=kLoop, calls=%fused_computation.262 | loop fusion | bytes 56623104 | tf_op jit(solution)/shard_map/jit(_roll_static)/concatenate | solution.py:105
  978.2 23.4 %fusion.148 = bf16[96,1,3,24,2,256]{5,3,4,2,0,1:T(8,128)(2,1)} fusion(f32[96]{0:T(128)S(1)} %sine_multiply_fusion, f32[96,1,24,768]{3,2,1,0:T(8,128)} %get-tuple-element.826, bf16[96,2,24,768]{3,2,1,0:T(8,128)(2,1)} %get-tuple-element.832, bf16[96,1,24,768]{3,2,1,0:T(8,128)(2,1)} %get-tuple-element.834, ...), kind=kOutput, calls=%fused_computation.294 | convolution fusion | flops 5518393344 | bytes 72352128 | tf_op jit(solution)/shard_map/ascvo,pmo->ascvpm/dot_general | solution.py:150
  1014.5 70.7 %all-to-all-done.1 = bf16[96,1,3,24,2,256]{0,3,4,2,1,5:T(8,128)(2,1)} async-done(((bf16[96,1,3,24,2,256]{0,3,4,2,1,5:T(8,128)(2,1)}), bf16[96,1,3,24,2,256]{0,3,4,2,1,5:T(8,128)(2,1)}, u32[]{:S(2)}, u32[]{:S(2)}) %all-to-all-start.1) | async-done | bytes 7077920 | tf_op jit(solution)/shard_map/all_to_all | solution.py:154
  1113.7 15.3 %concatenate.98 = bf16[384,1,3,24,2,32,2]{0,3,6,5,4,2,1:T(8,128)(2,1)} reshape(bf16[4,96,1,3,24,2,64]{1,0,4,6,5,3,2:T(4,128)(2,1)} %copy.153) | data formatting | bytes 14155776 | tf_op jit(solution)/shard_map/concatenate | solution.py:155
  1129.0 167.4 %all-to-all-done.3 = bf16[96,1,3,24,2,256]{0,3,4,2,1,5:T(8,128)(2,1)} async-done(((bf16[96,1,3,24,2,256]{0,3,4,2,1,5:T(8,128)(2,1)}), bf16[96,1,3,24,2,256]{0,3,4,2,1,5:T(8,128)(2,1)}, u32[]{:S(2)}, u32[]{:S(2)}) %all-to-all-start.3) | async-done | bytes 7077920 | tf_op jit(solution)/shard_map/all_to_all | solution.py:154
  1318.7 15.3 %concatenate.105 = bf16[384,1,3,24,2,32,2]{0,3,6,5,4,2,1:T(8,128)(2,1)} reshape(bf16[4,96,1,3,24,2,64]{1,0,4,6,5,3,2:T(4,128)(2,1)} %copy.163) | data formatting | bytes 14155776 | tf_op jit(solution)/shard_map/concatenate | solution.py:155
  1333.9 20.1 %fusion.120 = f32[2,3,24,2,32,257]{5,2,3,1,0,4:T(8,128)} fusion(f32[32,2,257]{2,1,0:T(2,128)S(1)} %copy-done.9, bf16[272,32,384]{2,0,1:T(8,128)(2,1)} %bitcast.213, bf16[384,1,3,24,2,32,2]{0,3,6,5,4,2,1:T(8,128)(2,1)} %concatenate.105, bf16[384,1,3,24,2,32,2]{0,3,6,5,4,2,1:T(8,128)(2,1)} %concatenate.98), kind=kOutput, calls=%fused_computation.251 | convolution fusion | flops 3652217856 | bytes 30183680 | tf_op jit(solution)/shard_map/ascvpqh,rqa->scvpqhr/dot_general | solution.py:157
  1354.0 18.2 %copy.166 = f32[2,3,24,2,32,257]{5,4,2,3,1,0:T(8,128)} copy(f32[2,3,24,2,32,257]{5,2,3,1,0,4:T(8,128)} %fusion.120) | data formatting | bytes 18948096 | tf_op jit(solution)/shard_map/reduce_sum | solution.py:160
  1372.2 14.5 %reshape.1597 = f32[1,2,3,24,2,8224]{5,3,4,2,1,0:T(8,128)} reshape(f32[2,3,24,2,32,257]{5,4,2,3,1,0:T(8,128)} %copy.166) | data formatting | bytes 18948096 | tf_op jit(solution)/shard_map/reshape | solution.py:160
  (625 shorter events, 375.4 us)
Async XLA Ops:
  274.8 12.7 copy-start.7
  274.8 8.3 slice-start
  274.8 8.3 slice-start.1
  287.5 18.0 %copy-start.12 = (f32[2]{0:T(128)S(1)}, f32[2]{0:T(128)}, u32[]{:S(2)}) copy-start(f32[2]{0:T(128)} %constant.378.clone) | copy-start | bytes 28
  394.5 6.6 copy-start
  394.5 162.3 %all-to-all-start = ((bf16[4,2,442368]{2,1,0:T(2,128)(2,1)}), bf16[4,2,442368]{2,1,0:T(2,128)(2,1)}, u32[]{:S(2)}, u32[]{:S(2)}) async-start(bf16[4,2,442368]{2,1,0:T(2,128)(2,1)} %reshape.1613), calls=%async_computation | async-start | bytes 14155776 | tf_op jit(solution)/shard_map/all_to_all | solution.py:143
  401.1 420.1 %all-gather.2.cloned.1.call-start = ((), (), s32[]{:S(2)}) async-start(), calls=%async_computation.4 | async-start | bytes 13271040 | tf_op jit(solution)/shard_map/all_gather | solution.py:135
  435.5 126.8 %copy-start.13 = (u32[32]{0:T(128)S(1)}, u32[32]{0:T(128)}, u32[]{:S(2)}) copy-start(u32[32]{0:T(128)} %constant.385) | copy-start | bytes 388
  435.5 128.1 %copy-start.10 = (s32[32]{0:T(128)S(1)}, s32[32]{0:T(128)}, u32[]{:S(2)}) copy-start(s32[32]{0:T(128)} %get-tuple-element.1309) | copy-start | bytes 388
  556.9 317.5 %all-to-all-start.2 = ((bf16[4,2,442368]{2,1,0:T(2,128)(2,1)}), bf16[4,2,442368]{2,1,0:T(2,128)(2,1)}, u32[]{:S(2)}, u32[]{:S(2)}) async-start(bf16[4,2,442368]{2,1,0:T(2,128)(2,1)} %reshape.1611), calls=%async_computation.2 | async-start | bytes 14155776 | tf_op jit(solution)/shard_map/all_to_all | solution.py:143
  720.7 55.9 %copy-start.1 = (f32[1,256,768]{2,1,0:T(8,128)}, f32[1,256,768]{2,1,0:T(8,128)S(1)}, u32[]{:S(2)}) copy-start(f32[1,256,768]{2,1,0:T(8,128)S(1)} %get-tuple-element.837) | copy-start | bytes 2359300
  720.7 55.9 %copy-start.4 = (f32[1,256,768]{2,1,0:T(8,128)}, f32[1,256,768]{2,1,0:T(8,128)S(1)}, u32[]{:S(2)}) copy-start(f32[1,256,768]{2,1,0:T(8,128)S(1)} %get-tuple-element.838) | copy-start | bytes 2359300
  832.0 6.0 copy-start.2
  832.0 6.0 copy-start.5
  874.3 210.9 %all-to-all-start.1 = ((bf16[96,1,3,24,2,256]{0,3,4,2,1,5:T(8,128)(2,1)}), bf16[96,1,3,24,2,256]{0,3,4,2,1,5:T(8,128)(2,1)}, u32[]{:S(2)}, u32[]{:S(2)}) async-start(bf16[96,1,3,24,2,256]{0,3,4,2,1,5:T(8,128)(2,1)} %copy.151), calls=%async_computation.1 | async-start | bytes 18874368 | tf_op jit(solution)/shard_map/all_to_all | solution.py:154
  959.2 19.0 %copy-start.3 = (f32[1,256,768]{2,1,0:T(8,128)S(1)}, f32[1,256,768]{2,1,0:T(8,128)}, u32[]{:S(2)}) copy-start(f32[1,256,768]{2,1,0:T(8,128)} %copy-done.1) | copy-start | bytes 2359300
  959.2 19.0 %copy-start.6 = (f32[1,256,768]{2,1,0:T(8,128)S(1)}, f32[1,256,768]{2,1,0:T(8,128)}, u32[]{:S(2)}) copy-start(f32[1,256,768]{2,1,0:T(8,128)} %copy-done.4) | copy-start | bytes 2359300
  1014.5 76.9 %copy-start.8 = (s32[32]{0:T(128)S(1)}, s32[32]{0:T(128)}, u32[]{:S(2)}) copy-start(s32[32]{0:T(128)} %copy-done.7) | copy-start | bytes 388
  1014.5 76.9 %copy-start.11 = (s32[32]{0:T(128)S(1)}, s32[32]{0:T(128)}, u32[]{:S(2)}) copy-start(s32[32]{0:T(128)} %get-tuple-element.1309) | copy-start | bytes 388
  1085.2 211.2 %all-to-all-start.3 = ((bf16[96,1,3,24,2,256]{0,3,4,2,1,5:T(8,128)(2,1)}), bf16[96,1,3,24,2,256]{0,3,4,2,1,5:T(8,128)(2,1)}, u32[]{:S(2)}, u32[]{:S(2)}) async-start(bf16[96,1,3,24,2,256]{0,3,4,2,1,5:T(8,128)(2,1)} %copy.161), calls=%async_computation.3 | async-start | bytes 18874368 | tf_op jit(solution)/shard_map/all_to_all | solution.py:154
  1318.7 15.3 %copy-start.9 = (f32[32,2,257]{2,1,0:T(2,128)S(1)}, f32[32,2,257]{2,1,0:T(2,128)}, u32[]{:S(2)}) copy-start(f32[32,2,257]{2,1,0:T(2,128)} %get-tuple-element.836) | copy-start | bytes 197380
Sparse Core Ops, SparseCore 0:
  403.5 72.8 all-gather.1
where the time goes:
time: 1420 us; the launch traced here: 1410 us
  local copies, waits for them, and re-layouts  464 us (33%)
  waiting for transfers between devices  360 us (25%)
  loops' own time  163 us (11%)
  blocking collectives  153 us (11%)
  matrix products  120 us (8%)
  other arithmetic  110 us (8%)
  starting transfers between devices  23.9 us (2%)
  between operations  15.2 us (1%)
    all_to_all x2, waiting for transfers between devices, shards(): lax.all_to_all(fourier, 'ma', split_axis=5, concat_axis=0, tiled=True)  238 us
    another operation x1, loops' own time, pair_table(): _, values = lax.scan(block_rows, (blank_rows, blank_rows), firsts)  163 us
    unnamed x1, blocking collectives  153 us
    all_to_all x2, waiting for transfers between devices, shards(): lax.all_to_all(spectra[:, test_id:test_id + 1], 'ma', split_axis=0, conca...  121 us
    concatenate x4, local copies, waits for them, and re-layouts, cross_field(): jnp.roll(magnetic, -2, along)  59.9 us
    unnamed x40, local copies, waits for them, and re-layouts  59.6 us
    all_to_all x4, local copies, waits for them, and re-layouts, shards(): lax.all_to_all(spectra[:, test_id:test_id + 1], 'ma', split_axis=0, conca...  59.2 us
    dot_general x2, matrix products, shards(): jnp.einsum('ascvo,pmo->ascvpm', emf, forward_table, preferred_element_typ...  46.7 us
  transfers between devices with their start and end apart: 5, of which 3 were waited for; matrix products, arithmetic and copies ran while one was open for 26% of the time, Pallas kernels for 0%

commit v1 on v0

--- a/solution.py
+++ b/solution.py
@@ -3,7 +3,9 @@
 import jax
 import jax.numpy as jnp
 from jax import lax
-from jax.sharding import PartitionSpec as P
+from jax.experimental import pallas as pl
+from jax.experimental.pallas import tpu as pltpu
+from jax.sharding import Mesh, PartitionSpec as P
 
 NM = 256
 NLAT = 384
@@ -107,7 +109,7 @@
     ) * jnp.roll(magnetic, -1, along)
 
 
-def shards(section, start, velocity, pair_list, wavenumber):
+def shards_general(section, start, velocity, pair_list, wavenumber):
     pair_count = pair_list.shape[0]
     leg_table, first_half, degree = pair_table(pair_list, NM, NLAT)
     legendre = leg_table.astype(jnp.bfloat16)
@@ -167,18 +169,346 @@
     return updated[None]
 
 
+BF16 = jnp.bfloat16
+F32 = jnp.float32
+VMEM_CAP = 56 << 20
+PAIR_ROWS = NM + 1
+CHUNK_ROWS = 16
+SLOTS = 8
+
+
+def table_window(slots):
+    return -(-(PAIR_ROWS + slots - 1) // 32) * 32
+
+
+def swap_major(block):
+    return jnp.swapaxes(block, 0, 1)
+
+
+def table_kernel(upper, lower, first, second, seed_low, seed_high, cosine, out):
+    shape = seed_low.shape
+    cosine_rows = jnp.broadcast_to(cosine[...], shape)
+    first_step = first[...]
+    second_step = second[...]
+    low_value = seed_low[...]
+    high_value = seed_high[...]
+
+    def chunk(index, state):
+        latest, before = state
+        scale_up = upper[index]
+        scale_down = lower[index]
+        produced = []
+        for offset in range(CHUNK_ROWS):
+            step = index * CHUNK_ROWS + offset
+            recurred = (scale_up[:, offset : offset + 1] * cosine_rows) * latest - scale_down[
+                :, offset : offset + 1
+            ] * before
+            current = jnp.where(
+                first_step == step,
+                low_value,
+                jnp.where(second_step == step, high_value, recurred),
+            )
+            produced.append(current)
+            latest, before = current, latest
+        rows = swap_major(jnp.stack(produced))
+        out[:, pl.ds(pl.multiple_of(index * CHUNK_ROWS, CHUNK_ROWS), CHUNK_ROWS), :] = rows.astype(
+            BF16
+        )
+        return latest, before
+
+    blank = jnp.zeros(shape, F32)
+    lax.fori_loop(0, out.shape[1] // CHUNK_ROWS, chunk, (blank, blank))
+
+
+def legendre_table(every_pair, slots, lats):
+    pairs = every_pair.shape[0]
+    window = table_window(slots)
+    order_low = every_pair.astype(F32)
+    order_high = (NM - 1 - every_pair).astype(F32)
+    colatitude = jnp.pi * (lats.astype(F32) + 0.5) / NLAT
+    seed_low = seed_values(order_low, NM, jnp.sin(colatitude))
+    seed_high = seed_values(order_high, NM, jnp.sin(colatitude))
+    slot = jnp.arange(pairs, dtype=jnp.int32) % slots
+    row = jnp.arange(window, dtype=jnp.int32)[None, :] - slot[:, None]
+    switch = NM - every_pair
+    in_low = row < switch[:, None]
+    degree = jnp.where(in_low, every_pair[:, None] + row, row - 1)
+    order = jnp.where(in_low, order_low[:, None], order_high[:, None])
+    real = degree.astype(F32)
+    active = (real > order) & (row >= 0) & (row < PAIR_ROWS)
+    divisor = jnp.where(active, real * real - order * order, 1.0)
+    upper = jnp.sqrt(jnp.maximum(4.0 * real * real - 1.0, 0.0) / divisor)
+    lower_num = ((real - 1.0) * (real - 1.0) - order * order) * (2.0 * real + 1.0)
+    lower = jnp.sqrt(
+        jnp.maximum(lower_num, 0.0) / (divisor * jnp.maximum(2.0 * real - 3.0, 1.0))
+    )
+    by_chunk = lambda values: jnp.swapaxes(
+        jnp.where(active, values, 0.0).reshape(pairs, window // CHUNK_ROWS, CHUNK_ROWS), 0, 1
+    )
+    spread_out = lambda values: jnp.broadcast_to(values[:, None], (pairs, NLAT))
+    chunks = window // CHUNK_ROWS
+    coefficient = pl.BlockSpec((chunks, 8, CHUNK_ROWS), lambda q: (0, q, 0))
+    per_pair = pl.BlockSpec((8, NLAT), lambda q: (q, 0))
+    return pl.pallas_call(
+        table_kernel,
+        grid=(pairs // 8,),
+        in_specs=[coefficient, coefficient, per_pair, per_pair, per_pair, per_pair]
+        + [pl.BlockSpec((1, NLAT), lambda q: (0, 0))],
+        out_specs=pl.BlockSpec((8, window, NLAT), lambda q: (q, 0, 0)),
+        out_shape=jax.ShapeDtypeStruct((pairs, window, NLAT), BF16),
+        compiler_params=pltpu.CompilerParams(vmem_limit_bytes=VMEM_CAP),
+        name="table",
+    )(
+        by_chunk(upper),
+        by_chunk(lower),
+        spread_out(slot),
+        spread_out(slot + switch),
+        seed_low,
+        seed_high,
+        jnp.cos(colatitude)[None, :],
+    )
+
+
+def synthesis_kernel(switch, spec, table, out):
+    source, group = pl.program_id(0), pl.program_id(1)
+    groups = pl.num_programs(1)
+    window = table.shape[1]
+    fields = spec.shape[1]
+    lane = lax.broadcasted_iota(jnp.int32, (fields, window), 1)
+    collected = []
+    for slot in range(SLOTS):
+        start = pl.multiple_of((group * SLOTS + slot) * NM, NM)
+        rows = spec[0, :, pl.ds(start, window)].astype(F32)
+        in_low = lane < switch[(source * groups + group) * SLOTS + slot]
+        both = jnp.concatenate([jnp.where(in_low, rows, 0.0), jnp.where(in_low, 0.0, rows)], axis=0)
+        made = jnp.dot(both.astype(BF16), table[slot], preferred_element_type=F32)
+        collected += [made[:fields], made[fields:]]
+    out[...] = swap_major(jnp.stack(collected)).astype(BF16)
+
+
+def synthesis(spec, table, switch, slots):
+    sources, fields, width = spec.shape
+    pairs, window, _ = table.shape
+    groups = slots // SLOTS
+    return pl.pallas_call(
+        synthesis_kernel,
+        grid_spec=pltpu.PrefetchScalarGridSpec(
+            num_scalar_prefetch=1,
+            grid=(sources, groups),
+            in_specs=[
+                pl.BlockSpec((1, fields, width), lambda z, g, _: (z, 0, 0)),
+                pl.BlockSpec((SLOTS, window, NLAT), lambda z, g, _: (z * groups + g, 0, 0)),
+            ],
+            out_specs=pl.BlockSpec(
+                (fields, 2 * SLOTS, NLAT), lambda z, g, _: (0, z * groups + g, 0)
+            ),
+        ),
+        out_shape=jax.ShapeDtypeStruct((fields, 2 * pairs, NLAT), BF16),
+        compiler_params=pltpu.CompilerParams(vmem_limit_bytes=VMEM_CAP),
+        name="synthesis",
+    )(switch, spec, table)
+
+
+LON_TILE = 256
+
+
+def grid_kernel(spectra, wind, inverse_cos, inverse_sin, forward_cos, forward_sin, weights, out, emf):
+    for tile in range(NLON // LON_TILE):
+        span = pl.ds(tile * LON_TILE, LON_TILE)
+        magnetic = [
+            jnp.dot(inverse_cos[span, :], spectra[2 * c], preferred_element_type=F32)
+            + jnp.dot(inverse_sin[span, :], spectra[2 * c + 1], preferred_element_type=F32)
+            for c in range(3)
+        ]
+        motion = [wind[c, span, :].astype(F32) for c in range(3)]
+        for c in range(3):
+            one, two = (c + 1) % 3, (c + 2) % 3
+            emf[c, span, :] = (
+                motion[one] * magnetic[two] - motion[two] * magnetic[one]
+            ).astype(BF16)
+    scale = weights[...]
+    for c in range(3):
+        for part, table in enumerate((forward_cos, forward_sin)):
+            back = jnp.dot(table[...], emf[c], preferred_element_type=F32)
+            out[2 * c + part] = (back * scale).astype(BF16)
+
+
+def grid_product(spectra, wind, tables, weights):
+    fields, orders, lats = spectra.shape
+    whole = lambda array: pl.BlockSpec(array.shape, lambda g: (0,) * array.ndim)
+    per_group = pl.BlockSpec((6, orders, lats), lambda g: (g, 0, 0))
+    return pl.pallas_call(
+        grid_kernel,
+        grid=(fields // 6,),
+        in_specs=[per_group, whole(wind)] + [whole(table) for table in tables] + [whole(weights)],
+        out_specs=per_group,
+        out_shape=jax.ShapeDtypeStruct(spectra.shape, BF16),
+        scratch_shapes=[pltpu.VMEM((3, NLON, lats), BF16)],
+        compiler_params=pltpu.CompilerParams(vmem_limit_bytes=VMEM_CAP),
+        name="grid_product",
+    )(spectra, wind, *tables, weights)
+
+
+def analysis_kernel(switch, fourier, table, out, carry):
+    source, group = pl.program_id(0), pl.program_id(1)
+    groups = pl.num_programs(1)
+    window = table.shape[1]
+    fields = fourier.shape[0]
+    lane = lax.broadcasted_iota(jnp.int32, (fields, window), 1)
+    by_order = swap_major(fourier[...].astype(F32)).astype(BF16)
+
+    @pl.when(group == 0)
+    def _():
+        carry[...] = jnp.zeros_like(carry)
+
+    over = carry[...]
+    blank = jnp.zeros((fields, 128 - (window - NM)), F32)
+    for slot in range(SLOTS):
+        both = jnp.concatenate([by_order[2 * slot], by_order[2 * slot + 1]], axis=0)
+        made = lax.dot_general(
+            both, table[slot], (((1,), (1,)), ((), ())), preferred_element_type=F32
+        )
+        in_low = lane < switch[(source * groups + group) * SLOTS + slot]
+        rows = jnp.where(in_low, made[:fields], made[fields:])
+        start = pl.multiple_of((group * SLOTS + slot) * NM, NM)
+        out[0, :, pl.ds(start, 128)] = (rows[:, :128] + over).astype(BF16)
+        out[0, :, pl.ds(start + 128, NM - 128)] = rows[:, 128:NM].astype(BF16)
+        over = jnp.concatenate([rows[:, NM:], blank], axis=1)
+    carry[...] = over
+
+    @pl.when(group == groups - 1)
+    def _():
+        width = out.shape[2]
+        full = width // NM * NM
+        out[0, :, full:] = over[:, : width - full].astype(BF16)
+
+
+def analysis(fourier, table, switch, slots, width):
+    fields, orders, lats = fourier.shape
+    pairs, window, _ = table.shape
+    groups = slots // SLOTS
+    return pl.pallas_call(
+        analysis_kernel,
+        grid_spec=pltpu.PrefetchScalarGridSpec(
+            num_scalar_prefetch=1,
+            grid=(pairs // slots, groups),
+            in_specs=[
+                pl.BlockSpec((fields, 2 * SLOTS, NLAT), lambda z, g, _: (0, z * groups + g, 0)),
+                pl.BlockSpec((SLOTS, window, NLAT), lambda z, g, _: (z * groups + g, 0, 0)),
+            ],
+            out_specs=pl.BlockSpec((1, fields, width), lambda z, g, _: (z, 0, 0)),
+            scratch_shapes=[pltpu.VMEM((fields, 128), F32)],
+        ),
+        out_shape=jax.ShapeDtypeStruct((pairs // slots, fields, width), BF16),
+        compiler_params=pltpu.CompilerParams(vmem_limit_bytes=VMEM_CAP),
+        name="analysis",
+    )(switch, fourier, table)
+
+
+def gather_pairs(pair_list, count):
+    own = pair_list.shape[0]
+    place = lax.axis_index("ma")
+    every = jnp.zeros((count, own), jnp.int32)
+    every = lax.dynamic_update_slice(every, pair_list[None], (place, 0))
+    for shift in range(1, count):
+        moved = lax.ppermute(pair_list, "ma", [(k, (k + shift) % count) for k in range(count)])
+        every = lax.dynamic_update_slice(every, moved[None], ((place - shift) % count, 0))
+    return every.reshape(-1)
+
+
+def shards_by_level(section, start, velocity, pair_list, wavenumber, *, count):
+    slots = pair_list.shape[0]
+    width = section.shape[-1]
+    depth = LEV // (2 * count)
+    band = velocity.shape[0]
+    half = band // 2
+    every_pair = gather_pairs(pair_list, count)
+    slot_of = jnp.arange(count * slots, dtype=jnp.int32) % slots
+    switch = slot_of + NM - every_pair
+
+    anchor = (pair_list == 0)[:, None] & (jnp.arange(PAIR_ROWS) == 0)[None, :]
+    anchor_rows = anchor.reshape(-1).astype(F32)
+    part_pick = jnp.array([1.0, 0.0], F32)
+    forcing = test_field(wavenumber[0], TESTS, LEV)
+    spec_field = (
+        section[0].astype(F32)
+        + forcing[:, :, :, None, None] * part_pick[:, None] * anchor_rows[None, :]
+    ).astype(BF16)
+    spec_field = spec_field.reshape(TESTS * 3, 2 * count, depth, 2, width)
+
+    split = velocity.reshape(2, half, 3, LEV // 4, NLON)
+    split = lax.all_to_all(split, "k", split_axis=0, concat_axis=0, tiled=True)
+    split = split.transpose(0, 3, 1, 2, 4).reshape(count, depth, half, 3, NLON)
+
+    lats = jnp.arange(NLAT, dtype=jnp.int32).reshape(count, 2, half).swapaxes(0, 1).reshape(-1)
+    table = legendre_table(every_pair, slots, lats)
+    order_list = jnp.stack([every_pair, NM - 1 - every_pair], axis=1).reshape(-1)
+    waves = wave_table(order_list, NLON)
+    inverse_table = (waves * grid_scale).astype(BF16)
+    forward_table = (waves * (2.0 * jnp.pi / NLON)).astype(BF16)
+    tables = (inverse_table[0].T, inverse_table[1].T, forward_table[0], forward_table[1])
+    weights = lat_weights(lats, NLAT)[None, :]
+
+    across = lax.axis_index("x")
+    core = lax.axis_index("k")
+    own_first = (across == 0) & (core == 0)
+    own_second = (across == 1) & (core == 1)
+    returned = []
+    for level in range(depth):
+        sent = spec_field[:, :, level].swapaxes(0, 1)
+        arrived = lax.all_to_all(sent, ("k", "ma"), split_axis=0, concat_axis=0, tiled=True)
+        spec = arrived.reshape(2, count, TESTS * 6, width).swapaxes(0, 1)
+        spec = spec.reshape(count, TESTS * 12, width)
+        spectra = synthesis(spec, table, switch, slots)
+
+        held = lax.all_to_all(split[:, level], "ma", split_axis=0, concat_axis=0, tiled=True)
+        turn = lax.ppermute(held, ("x", "k"), [(0, 2), (1, 0), (2, 3), (3, 1)])
+        cross = lax.ppermute(held, ("x", "k"), [(1, 2), (2, 1)])
+        first = jnp.where(own_first, held, jnp.where((across == 0) & (core == 1), cross, turn))
+        second = jnp.where(own_second, held, jnp.where((across == 1) & (core == 0), cross, turn))
+        wind = jnp.stack([first, second]).reshape(NLAT, 3, NLON).transpose(1, 2, 0)
+
+        fourier = grid_product(spectra, wind, tables, weights)
+        tendency = analysis(fourier, table, switch, slots, width)
+        back = tendency.reshape(count, 2, TESTS * 3, 2, width).swapaxes(0, 1)
+        back = back.reshape(2 * count, TESTS * 3, 2, width)
+        returned.append(
+            lax.all_to_all(back, ("k", "ma"), split_axis=0, concat_axis=0, tiled=True)
+        )
+    tendency = jnp.stack(returned, axis=1).reshape(LEV, TESTS, 3, 2, width)
+    tendency = tendency.transpose(1, 2, 0, 3, 4).astype(F32)
+
+    row_index = jnp.arange(PAIR_ROWS, dtype=jnp.int32)
+    first_half = row_index[None, :] < (NM - pair_list)[:, None]
+    degree = jnp.where(first_half, pair_list[:, None] + row_index[None, :], row_index[None, :] - 1)
+    spread = (degree * (degree + 1)).astype(F32).reshape(-1)
+    updated = start[0] + step_weight * (tendency - diffusion * spread * section[0].astype(F32))
+    return updated[None]
+
+
 def solution(mesh):
+    sizes = dict(mesh.shape)
+    count = sizes["ma"]
+    whole_slots = (NM // 2) % (count * SLOTS) == 0
+    if sizes["team"] == 4 and LEV % (2 * count) == 0 and whole_slots:
+        grid = Mesh(
+            mesh.devices.reshape(sizes["run"], 2, 2, count), ("run", "x", "k", "ma")
+        )
+        team = ("x", "k")
+        body = lambda *arrays: shards_by_level(*arrays, count=count)
+    else:
+        grid, team, body = mesh, ("team",), shards_general
     placed = (
-        P(("run", "team"), None, None, None, None, "ma"),
-        P(("run", "team"), None, None, None, None, "ma"),
-        P(("run", "ma"), None, "team", None),
+        P(("run",) + team, None, None, None, None, "ma"),
+        P(("run",) + team, None, None, None, None, "ma"),
+        P(("run", "ma"), None, team, None),
         P("ma"),
-        P("team"),
+        P(team),
     )
     return jax.shard_map(
-        shards,
-        mesh=mesh,
+        body,
+        mesh=grid,
         in_specs=placed,
-        out_specs=P(("run", "team"), None, None, None, None, "ma"),
+        out_specs=P(("run",) + team, None, None, None, None, "ma"),
         check_vma=False,
     )

time: 1420 us -> 591 us (0.42)
  local copies, waits for them, and re-layouts: 464 us -> 75.6 us
  Pallas kernels: 0 us -> 222 us
  waiting for transfers between devices: 360 us -> 142 us
  loops' own time: 163 us -> 0 us
  matrix products: 120 us -> 0 us
  blocking collectives: 153 us -> 47.3 us
  other arithmetic: 110 us -> 38.3 us
  starting transfers between devices: 23.9 us -> 54.7 us
    all_to_all x4 -> x8, waiting for transfers between devices: 360 us -> 76.8 us  [the longest x3 43.2 us: shards_by_level(): lax.all_to_all(split[:, level], 'ma', split_axis=0, concat_axis=0, tiled=...]
    pallas_call x0 -> x10, Pallas kernels: none -> 222 us  [the longest x3 68.8 us: analysis(): pl.pallas_call(analysis_kernel, grid_spec=pltpu.PrefetchScalarGridSpec(nu...]
    another operation x1 -> x0, loops' own time: 163 us -> none  [pair_table(): _, values = lax.scan(block_rows, (blank_rows, blank_rows), firsts)]
    unnamed x1 -> x0, blocking collectives: 153 us -> none
    dot_general x6 -> x0, matrix products: 120 us -> none  [the longest x2 46.7 us: shards(): jnp.einsum('ascvo,pmo->ascvpm', emf, forward_table, preferred_element_typ...]
    concatenate x8 -> x0, local copies, waits for them, and re-layouts: 98.6 us -> none  [the longest x4 59.9 us: cross_field(): jnp.roll(magnetic, -2, along)]
    all_to_all x8 -> x7, local copies, waits for them, and re-layouts: 103 us -> 8.84 us  [the longest x3 5.36 us: shards_by_level(): lax.all_to_all(back, ('k', 'ma'), split_axis=0, concat_axis=0, tiled=True)]
    ppermute x0 -> x9, waiting for transfers between devices: none -> 65.3 us  [the longest x3 34.5 us: shards_by_level(): turn = lax.ppermute(held, ('x', 'k'), [(0, 2), (1, 0), (2, 3), (3, 1)])]
  transfers between devices with their start and end apart: 5 -> 17, of which waited for: 3 -> 8; matrix products, arithmetic and copies ran while one was open for 26% -> 14% of each run, Pallas kernels for 0% -> 38%
where the time goes in v1:
time: 591 us; the launch traced here: 582 us
  Pallas kernels  222 us (38%)
  waiting for transfers between devices  142 us (24%)
  local copies, waits for them, and re-layouts  75.6 us (13%)
  starting transfers between devices  54.7 us (9%)
  blocking collectives  47.3 us (8%)
  other arithmetic  38.3 us (6%)
    pallas_call x3, Pallas kernels, analysis(): pl.pallas_call(analysis_kernel, grid_spec=pltpu.PrefetchScalarGridSpec(nu...  68.8 us
    pallas_call x3, Pallas kernels, synthesis(): pl.pallas_call(synthesis_kernel, grid_spec=pltpu.PrefetchScalarGridSpec(n...  60.3 us
    pallas_call x1, Pallas kernels, legendre_table(): pl.pallas_call(table_kernel, grid=(pairs // 8,), in_specs=[coefficient, c...  48.9 us
    pallas_call x3, Pallas kernels, grid_product(): pl.pallas_call(grid_kernel, grid=(fields // 6,), in_specs=[per_group, who...  44.3 us
    all_to_all x3, waiting for transfers between devices, shards_by_level(): lax.all_to_all(split[:, level], 'ma', split_axis=0, concat_axis=0, tiled=...  43.2 us
    all_to_all x1, blocking collectives, shards_by_level(): lax.all_to_all(sent, ('k', 'ma'), split_axis=0, concat_axis=0, tiled=True)  41.4 us
    ppermute x3, waiting for transfers between devices, shards_by_level(): turn = lax.ppermute(held, ('x', 'k'), [(0, 2), (1, 0), (2, 3), (3, 1)])  34.5 us
    all_to_all x3, waiting for transfers between devices, shards_by_level(): lax.all_to_all(back, ('k', 'ma'), split_axis=0, concat_axis=0, tiled=True)  33.6 us
  transfers between devices with their start and end apart: 17, of which 8 were waited for; matrix products, arithmetic and copies ran while one was open for 14% of the time, Pallas kernels for 38%

profile of v1, /device:TPU:0, one launch (start us, length us, event | category | flops | bytes accessed | tf_op | source)
XLA Modules:
  0.0 581.8 jit_solution(17033422246124414497)
XLA Ops:
  17.3 7.2 %copy_convert_fusion = f32[1,2,3,24,2,8224]{5,4,2,1,3,0:T(2,128)} fusion(bf16[1,2,3,24,2,8224]{5,4,3,2,1,0:T(2,128)(2,1)} %param.6), kind=kLoop, calls=%fused_computation.8 | loop fusion | flops 2368512 | bytes 14211072 | tf_op jit(solution)/shard_map/convert_element_type | solution.py:434
  24.5 14.1 %all-to-all-done.2 = bf16[4,48,3,768]{3,1,2,0:T(8,128)(2,1)S(1)} async-done(((bf16[4,48,3,768]{3,1,2,0:T(8,128)(2,1)}), bf16[4,48,3,768]{3,1,2,0:T(8,128)(2,1)S(1)}, u32[]{:S(2)}, u32[]{:S(2)}) %all-to-all-start.2) | async-done | bytes 884768 | tf_op jit(solution)/shard_map/all_to_all | solution.py:464
  43.1 7.9 %fusion.4 = bf16[6,8,3,2,8224]{4,3,0,1,2:T(2,128)(2,1)} fusion(f32[6,8,3,2,8224]{4,3,0,2,1:T(2,128)} %bitcast.116, f32[8224]{0:T(1024)S(1)} %reshape.580, f32[6,8,3,2]{3,0,1,2:T(8,128)S(1)} %broadcast_multiply_fusion), kind=kLoop, calls=%fused_computation.6 | loop fusion | flops 7105536 | bytes 14245120 | tf_op jit(solution)/shard_map/convert_element_type | solution.py:436
  51.0 13.8 %all-to-all-done.5 = bf16[4,48,3,768]{3,1,2,0:T(8,128)(2,1)S(1)} async-done(((bf16[4,48,3,768]{3,1,2,0:T(8,128)(2,1)}), bf16[4,48,3,768]{3,1,2,0:T(8,128)(2,1)S(1)}, u32[]{:S(2)}, u32[]{:S(2)}) %all-to-all-start.5) | async-done | bytes 884768 | tf_op jit(solution)/shard_map/all_to_all | solution.py:464
  75.5 15.4 %all-to-all-done.8 = bf16[4,48,3,768]{3,1,2,0:T(8,128)(2,1)S(1)} async-done(((bf16[4,48,3,768]{3,1,2,0:T(8,128)(2,1)}), bf16[4,48,3,768]{3,1,2,0:T(8,128)(2,1)S(1)}, u32[]{:S(2)}, u32[]{:S(2)}) %all-to-all-start.8) | async-done | bytes 884768 | tf_op jit(solution)/shard_map/all_to_all | solution.py:464
  90.9 41.4 %all_to_all.51 = bf16[8,6,2,8224]{3,2,1,0:T(2,128)(2,1)} all-to-all(bf16[8,6,2,8224]{3,2,1,0:T(2,128)(2,1)S(1)} %get-tuple-element.7), channel_id=1, replica_groups=mesh['run'=2,'x'=2,'k'=2,'ma'=4] {'k','ma'}, dimensions={0} | all-to-all | bytes 3158016 | tf_op jit(solution)/shard_map/all_to_all | solution.py:459
  143.3 23.3 %collective-permute-done = s32[32]{0:T(128)S(1)} collective-permute-done((s32[32]{0:T(128)S(1)}, s32[32]{0:T(128)S(1)}, u32[]{:S(2)}, u32[]{:S(2)}) %collective-permute-start) | collective-permute-done | bytes 160 | tf_op jit(solution)/shard_map/ppermute | solution.py:414
  166.7 7.5 %collective-permute-done.1 = s32[32]{0:T(128)S(1)} collective-permute-done((s32[32]{0:T(128)S(1)}, s32[32]{0:T(128)S(1)}, u32[]{:S(2)}, u32[]{:S(2)}) %collective-permute-start.1) | collective-permute-done | bytes 160 | tf_op jit(solution)/shard_map/ppermute | solution.py:414
  198.7 48.9 %table.1 = bf16[128,288,384]{2,1,0:T(8,128)(2,1)} custom-call(f32[18,128,16]{2,1,0:T(8,128)} %get-tuple-element.26.upper, f32[18,128,16]{2,1,0:T(8,128)} %get-tuple-element.25.lower, s32[128,384]{1,0:T(8,128)} %broadcast_in_dim.66.first, s32[128,384]{1,0:T(8,128)} %broadcast_in_dim.67.second, f32[128,384]{1,0:T(8,128)} %get-tuple-element.28.seed_low, ...), custom_call_target="tpu_custom_call" | custom-call | tf_op jit(solution)/shard_map/table/pallas_call | solution.py:252
  258.3 20.1 %synthesis.3.spectra = bf16[24,256,384]{2,1,0:T(8,128)(2,1)} custom-call(s32[128]{0:T(128)} %get-tuple-element.37.switch, bf16[4,24,8224]{2,1,0:T(8,128)(2,1)} %copy.181.spec, bf16[128,288,384]{2,1,0:T(8,128)(2,1)} %table.1), custom_call_target="tpu_custom_call" | custom-call | tf_op jit(solution)/shard_map/synthesis/pallas_call | solution.py:293
  278.4 14.8 %grid_product.3.fourier = bf16[24,256,384]{2,1,0:T(8,128)(2,1)} custom-call(bf16[24,256,384]{2,1,0:T(8,128)(2,1)} %synthesis.3.spectra, bf16[3,768,384]{2,1,0:T(8,128)(2,1)} %bitcast.126, bf16[768,256]{1,0:T(8,128)(2,1)} %copy.188.inverse_cos, bf16[768,256]{1,0:T(8,128)(2,1)} %copy.189.inverse_sin, bf16[256,768]{1,0:T(8,128)(2,1)} %get-tuple-element.22.forward_cos, ...), custom_call_target="tpu_custom_call" | custom-call | tf_op jit(solution)/shard_map/grid_product/pallas_call | solution.py:340
  293.1 22.9 %analysis.3 = bf16[4,24,8224]{2,1,0:T(8,128)(2,1)} custom-call(s32[128]{0:T(128)} %get-tuple-element.37.switch, bf16[24,256,384]{2,1,0:T(8,128)(2,1)} %grid_product.3.fourier, bf16[128,288,384]{2,1,0:T(8,128)(2,1)} %table.1), custom_call_target="tpu_custom_call" | custom-call | tf_op jit(solution)/shard_map/analysis/pallas_call | solution.py:390
  332.7 17.1 %collective-permute-done.6 = bf16[4,48,3,768]{3,1,2,0:T(8,128)(2,1)S(1)} collective-permute-done((bf16[4,48,3,768]{3,1,2,0:T(8,128)(2,1)S(1)}, bf16[4,48,3,768]{3,1,2,0:T(8,128)(2,1)S(1)}, u32[]{:S(2)}, u32[]{:S(2)}) %collective-permute-start.6) | collective-permute-done | bytes 884768 | tf_op jit(solution)/shard_map/ppermute | solution.py:465
  349.9 17.3 %collective-permute-done.8 = bf16[4,48,3,768]{3,1,2,0:T(8,128)(2,1)S(1)} collective-permute-done((bf16[4,48,3,768]{3,1,2,0:T(8,128)(2,1)S(1)}, bf16[4,48,3,768]{3,1,2,0:T(8,128)(2,1)S(1)}, u32[]{:S(2)}, u32[]{:S(2)}) %collective-permute-start.8) | collective-permute-done | bytes 884768 | tf_op jit(solution)/shard_map/ppermute | solution.py:465
  373.9 20.1 %synthesis.4.spectra = bf16[24,256,384]{2,1,0:T(8,128)(2,1)} custom-call(s32[128]{0:T(128)} %get-tuple-element.37.switch, bf16[4,24,8224]{2,1,0:T(8,128)(2,1)} %copy.194.spec, bf16[128,288,384]{2,1,0:T(8,128)(2,1)} %table.1), custom_call_target="tpu_custom_call" | custom-call | tf_op jit(solution)/shard_map/synthesis/pallas_call | solution.py:293
  394.0 14.8 %grid_product.4.fourier = bf16[24,256,384]{2,1,0:T(8,128)(2,1)} custom-call(bf16[24,256,384]{2,1,0:T(8,128)(2,1)} %synthesis.4.spectra, bf16[3,768,384]{2,1,0:T(8,128)(2,1)} %bitcast.127, bf16[768,256]{1,0:T(8,128)(2,1)} %copy.188.inverse_cos, bf16[768,256]{1,0:T(8,128)(2,1)} %copy.189.inverse_sin, bf16[256,768]{1,0:T(8,128)(2,1)} %get-tuple-element.22.forward_cos, ...), custom_call_target="tpu_custom_call" | custom-call | tf_op jit(solution)/shard_map/grid_product/pallas_call | solution.py:340
  408.7 22.9 %analysis.4 = bf16[4,24,8224]{2,1,0:T(8,128)(2,1)} custom-call(s32[128]{0:T(128)} %get-tuple-element.37.switch, bf16[24,256,384]{2,1,0:T(8,128)(2,1)} %grid_product.4.fourier, bf16[128,288,384]{2,1,0:T(8,128)(2,1)} %table.1), custom_call_target="tpu_custom_call" | custom-call | tf_op jit(solution)/shard_map/analysis/pallas_call | solution.py:390
  436.4 6.6 %all-to-all-start.6 = ((bf16[8,6,2,8224]{3,2,1,0:T(2,128)(2,1)}), bf16[8,6,2,8224]{3,2,1,0:T(2,128)(2,1)S(1)}, u32[]{:S(2)}, u32[]{:S(2)}) async-start(bf16[8,6,2,8224]{3,2,1,0:T(2,128)(2,1)} %bitcast.38), calls=%async_computation.6 | async-start | bytes 3194880 | tf_op jit(solution)/shard_map/all_to_all | solution.py:476
  452.3 20.1 %synthesis.5.spectra = bf16[24,256,384]{2,1,0:T(8,128)(2,1)} custom-call(s32[128]{0:T(128)} %get-tuple-element.37.switch, bf16[4,24,8224]{2,1,0:T(8,128)(2,1)} %copy.204.spec, bf16[128,288,384]{2,1,0:T(8,128)(2,1)} %table.1), custom_call_target="tpu_custom_call" | custom-call | tf_op jit(solution)/shard_map/synthesis/pallas_call | solution.py:293
  472.4 14.8 %grid_product.5.fourier = bf16[24,256,384]{2,1,0:T(8,128)(2,1)} custom-call(bf16[24,256,384]{2,1,0:T(8,128)(2,1)} %synthesis.5.spectra, bf16[3,768,384]{2,1,0:T(8,128)(2,1)} %bitcast.125, bf16[768,256]{1,0:T(8,128)(2,1)} %copy.188.inverse_cos, bf16[768,256]{1,0:T(8,128)(2,1)} %copy.189.inverse_sin, bf16[256,768]{1,0:T(8,128)(2,1)} %get-tuple-element.22.forward_cos, ...), custom_call_target="tpu_custom_call" | custom-call | tf_op jit(solution)/shard_map/grid_product/pallas_call | solution.py:340
  487.1 22.9 %analysis.5 = bf16[4,24,8224]{2,1,0:T(8,128)(2,1)} custom-call(s32[128]{0:T(128)} %get-tuple-element.37.switch, bf16[24,256,384]{2,1,0:T(8,128)(2,1)} %grid_product.5.fourier, bf16[128,288,384]{2,1,0:T(8,128)(2,1)} %table.1), custom_call_target="tpu_custom_call" | custom-call | tf_op jit(solution)/shard_map/analysis/pallas_call | solution.py:390
  524.2 33.6 %all-to-all-done.9 = bf16[8,6,2,8224]{3,2,1,0:T(2,128)(2,1)S(1)} async-done(((bf16[8,6,2,8224]{3,2,1,0:T(2,128)(2,1)}), bf16[8,6,2,8224]{3,2,1,0:T(2,128)(2,1)S(1)}, u32[]{:S(2)}, u32[]{:S(2)}) %all-to-all-start.9) | async-done | bytes 1579040 | tf_op jit(solution)/shard_map/all_to_all | solution.py:476
  561.6 7.1 %copy.211 = f32[8,3,6,2,8224]{4,3,2,1,0:T(2,128)S(1)} copy(f32[8,3,6,2,8224]{4,0,3,2,1:T(8,128)S(1)} %maximum_convert_fusion) | data formatting | bytes 18948096 | tf_op jit(solution)/shard_map/convert_element_type | solution.py:479
  568.7 8.2 %fusion.3 = f32[1,2,3,24,2,8224]{5,4,2,1,3,0:T(2,128)S(1)} fusion(f32[2,3,24,2,8224]{4,3,1,0,2:T(2,128)S(1)} %bitcast.115, f32[1,2,3,24,2,8224]{5,4,3,2,1,0:T(2,128)S(1)} %bitcast.121, f32[8224]{0:T(1024)S(1)} %fusion.38, bf16[1,2,3,24,2,8224]{5,4,3,2,1,0:T(2,128)(2,1)S(1)} %bitcast.118), kind=kLoop, calls=%fused_computation.4 | loop fusion | flops 11842560 | bytes 33192064 | tf_op jit(solution)/shard_map/broadcast_in_dim | solution.py:486
  (143 shorter events, 137.5 us)
Async XLA Ops:
  9.6 7.6 %copy-start.10 = (f32[2]{0:T(128)S(1)}, f32[2]{0:T(128)}, u32[]{:S(2)}) copy-start(f32[2]{0:T(128)} %constant.155.clone) | copy-start | bytes 28
  9.6 29.0 %all-to-all-start.2 = ((bf16[4,48,3,768]{3,1,2,0:T(8,128)(2,1)}), bf16[4,48,3,768]{3,1,2,0:T(8,128)(2,1)S(1)}, u32[]{:S(2)}, u32[]{:S(2)}) async-start(bf16[4,48,3,768]{3,1,2,0:T(8,128)(2,1)} %get-tuple-element.12), calls=%async_computation.2 | async-start | bytes 1769472 | tf_op jit(solution)/shard_map/all_to_all | solution.py:464
  39.6 25.2 %all-to-all-start.5 = ((bf16[4,48,3,768]{3,1,2,0:T(8,128)(2,1)}), bf16[4,48,3,768]{3,1,2,0:T(8,128)(2,1)S(1)}, u32[]{:S(2)}, u32[]{:S(2)}) async-start(bf16[4,48,3,768]{3,1,2,0:T(8,128)(2,1)} %get-tuple-element.14), calls=%async_computation.5 | async-start | bytes 1769472 | tf_op jit(solution)/shard_map/all_to_all | solution.py:464
  65.7 25.2 %all-to-all-start.8 = ((bf16[4,48,3,768]{3,1,2,0:T(8,128)(2,1)}), bf16[4,48,3,768]{3,1,2,0:T(8,128)(2,1)S(1)}, u32[]{:S(2)}, u32[]{:S(2)}) async-start(bf16[4,48,3,768]{3,1,2,0:T(8,128)(2,1)} %get-tuple-element.13), calls=%async_computation.8 | async-start | bytes 1769472 | tf_op jit(solution)/shard_map/all_to_all | solution.py:464
  90.9 41.5 %copy-start.5 = (bf16[4,48,3,768]{3,1,2,0:T(8,128)(2,1)}, bf16[4,48,3,768]{3,1,2,0:T(8,128)(2,1)S(1)}, u32[]{:S(2)}) copy-start(bf16[4,48,3,768]{3,1,2,0:T(8,128)(2,1)S(1)} %all-to-all-done.8) | copy-start | bytes 2654212
  132.4 42.0 %all-to-all-start.4 = ((bf16[8,6,2,8224]{3,2,1,0:T(2,128)(2,1)}), bf16[8,6,2,8224]{3,2,1,0:T(2,128)(2,1)S(1)}, u32[]{:S(2)}, u32[]{:S(2)}) async-start(bf16[8,6,2,8224]{3,2,1,0:T(2,128)(2,1)} %get-tuple-element.9), calls=%async_computation.4 | async-start | bytes 3194880 | tf_op jit(solution)/shard_map/all_to_all | solution.py:459
  135.9 30.7 %collective-permute-start = (s32[32]{0:T(128)S(1)}, s32[32]{0:T(128)S(1)}, u32[]{:S(2)}, u32[]{:S(2)}) collective-permute-start(s32[32]{0:T(128)S(1)} %copy-done.9), channel_id=1, source_target_pairs={{0,1},{1,2},{2,3},{3,0},{4,5},{5,6},{6,7},{7,4},{8,9},{9,10},{10,1... | collective-permute-start | bytes 392 | tf_op jit(solution)/shard_map/ppermute | solution.py:414
  137.9 36.4 %collective-permute-start.1 = (s32[32]{0:T(128)S(1)}, s32[32]{0:T(128)S(1)}, u32[]{:S(2)}, u32[]{:S(2)}) collective-permute-start(s32[32]{0:T(128)S(1)} %copy-done.9), channel_id=1, source_target_pairs={{0,2},{1,3},{2,0},{3,1},{4,6},{5,7},{6,4},{7,5},{8,10},{9,11},{10,... | collective-permute-start | bytes 392 | tf_op jit(solution)/shard_map/ppermute | solution.py:414
  140.2 34.0 %collective-permute-start.2 = (s32[32]{0:T(128)S(1)}, s32[32]{0:T(128)S(1)}, u32[]{:S(2)}, u32[]{:S(2)}) collective-permute-start(s32[32]{0:T(128)S(1)} %copy-done.9), channel_id=1, source_target_pairs={{0,3},{1,0},{2,1},{3,2},{4,7},{5,4},{6,5},{7,6},{8,11},{9,8},{10,9... | collective-permute-start | bytes 392 | tf_op jit(solution)/shard_map/ppermute | solution.py:414
  174.4 146.4 %all-to-all-start.7 = ((bf16[8,6,2,8224]{3,2,1,0:T(2,128)(2,1)}), bf16[8,6,2,8224]{3,2,1,0:T(2,128)(2,1)}, u32[]{:S(2)}, u32[]{:S(2)}) async-start(bf16[8,6,2,8224]{3,2,1,0:T(2,128)(2,1)} %get-tuple-element.8), calls=%async_computation.7 | async-start | bytes 3194880 | tf_op jit(solution)/shard_map/all_to_all | solution.py:459
  185.0 62.6 %collective-permute-start.3 = (bf16[4,48,3,768]{3,1,2,0:T(8,128)(2,1)S(1)}, bf16[4,48,3,768]{3,1,2,0:T(8,128)(2,1)S(1)}, u32[]{:S(2)}, u32[]{:S(2)}) collective-permute-start(bf16[4,48,3,768]{3,1,2,0:T(8,128)(2,1)S(1)} %copy-done.8), channel_id=1, source_target_pairs={{4,8},{8,4},{5,9},{9,5},{6,10},{10,6},{7,11},{11,7},{20,24},{24,20... | collective-permute-start | bytes 2654216 | tf_op jit(solution)/shard_map/ppermute | solution.py:466
  185.9 61.7 %collective-permute-start.4 = (bf16[4,48,3,768]{3,1,2,0:T(8,128)(2,1)S(1)}, bf16[4,48,3,768]{3,1,2,0:T(8,128)(2,1)}, u32[]{:S(2)}, u32[]{:S(2)}) collective-permute-start(bf16[4,48,3,768]{3,1,2,0:T(8,128)(2,1)S(1)} %copy-done.8), channel_id=1, source_target_pairs={{0,8},{4,0},{8,12},{12,4},{1,9},{5,1},{9,13},{13,5},{2,10},{6,2},{... | collective-permute-start | bytes 2654216 | tf_op jit(solution)/shard_map/ppermute | solution.py:465
  320.8 8.9 %copy-start.6 = (bf16[4,48,3,768]{3,1,2,0:T(8,128)(2,1)S(1)}, bf16[4,48,3,768]{3,1,2,0:T(8,128)(2,1)}, u32[]{:S(2)}) copy-start(bf16[4,48,3,768]{3,1,2,0:T(8,128)(2,1)} %copy-done.5) | copy-start | bytes 2654212
  320.8 115.6 %all-to-all-start.3 = ((bf16[8,6,2,8224]{3,2,1,0:T(2,128)(2,1)}), bf16[8,6,2,8224]{3,2,1,0:T(2,128)(2,1)}, u32[]{:S(2)}, u32[]{:S(2)}) async-start(bf16[8,6,2,8224]{3,2,1,0:T(2,128)(2,1)} %bitcast.26), calls=%async_computation.3 | async-start | bytes 3194880 | tf_op jit(solution)/shard_map/all_to_all | solution.py:476
  325.7 7.0 %collective-permute-start.5 = (bf16[4,48,3,768]{3,1,2,0:T(8,128)(2,1)S(1)}, bf16[4,48,3,768]{3,1,2,0:T(8,128)(2,1)S(1)}, u32[]{:S(2)}, u32[]{:S(2)}) collective-permute-start(bf16[4,48,3,768]{3,1,2,0:T(8,128)(2,1)S(1)} %copy-done.4), channel_id=1, source_target_pairs={{4,8},{8,4},{5,9},{9,5},{6,10},{10,6},{7,11},{11,7},{20,24},{24,20... | collective-permute-start | bytes 2654216 | tf_op jit(solution)/shard_map/ppermute | solution.py:466
  326.4 23.4 %collective-permute-start.6 = (bf16[4,48,3,768]{3,1,2,0:T(8,128)(2,1)S(1)}, bf16[4,48,3,768]{3,1,2,0:T(8,128)(2,1)S(1)}, u32[]{:S(2)}, u32[]{:S(2)}) collective-permute-start(bf16[4,48,3,768]{3,1,2,0:T(8,128)(2,1)S(1)} %copy-done.4), channel_id=1, source_target_pairs={{0,8},{4,0},{8,12},{12,4},{1,9},{5,1},{9,13},{13,5},{2,10},{6,2},{... | collective-permute-start | bytes 2654216 | tf_op jit(solution)/shard_map/ppermute | solution.py:465
  329.8 20.1 %collective-permute-start.7 = (bf16[4,48,3,768]{3,1,2,0:T(8,128)(2,1)S(1)}, bf16[4,48,3,768]{3,1,2,0:T(8,128)(2,1)S(1)}, u32[]{:S(2)}, u32[]{:S(2)}) collective-permute-start(bf16[4,48,3,768]{3,1,2,0:T(8,128)(2,1)S(1)} %copy-done.6), channel_id=1, source_target_pairs={{4,8},{8,4},{5,9},{9,5},{6,10},{10,6},{7,11},{11,7},{20,24},{24,20... | collective-permute-start | bytes 2654216 | tf_op jit(solution)/shard_map/ppermute | solution.py:466
  330.7 36.5 %collective-permute-start.8 = (bf16[4,48,3,768]{3,1,2,0:T(8,128)(2,1)S(1)}, bf16[4,48,3,768]{3,1,2,0:T(8,128)(2,1)S(1)}, u32[]{:S(2)}, u32[]{:S(2)}) collective-permute-start(bf16[4,48,3,768]{3,1,2,0:T(8,128)(2,1)S(1)} %copy-done.6), channel_id=1, source_target_pairs={{0,8},{4,0},{8,12},{12,4},{1,9},{5,1},{9,13},{13,5},{2,10},{6,2},{... | collective-permute-start | bytes 2654216 | tf_op jit(solution)/shard_map/ppermute | solution.py:465
  436.4 78.4 %all-to-all-start.6 = ((bf16[8,6,2,8224]{3,2,1,0:T(2,128)(2,1)}), bf16[8,6,2,8224]{3,2,1,0:T(2,128)(2,1)S(1)}, u32[]{:S(2)}, u32[]{:S(2)}) async-start(bf16[8,6,2,8224]{3,2,1,0:T(2,128)(2,1)} %bitcast.38), calls=%async_computation.6 | async-start | bytes 3194880 | tf_op jit(solution)/shard_map/all_to_all | solution.py:476
  514.8 43.0 %all-to-all-start.9 = ((bf16[8,6,2,8224]{3,2,1,0:T(2,128)(2,1)}), bf16[8,6,2,8224]{3,2,1,0:T(2,128)(2,1)S(1)}, u32[]{:S(2)}, u32[]{:S(2)}) async-start(bf16[8,6,2,8224]{3,2,1,0:T(2,128)(2,1)} %bitcast.51), calls=%async_computation.9 | async-start | bytes 3194880 | tf_op jit(solution)/shard_map/all_to_all | solution.py:476
  524.2 34.9 %copy-start = (bf16[8,6,2,8224]{3,0,2,1:T(8,128)(2,1)S(1)}, bf16[8,6,2,8224]{3,0,2,1:T(8,128)(2,1)}, u32[]{:S(2)}) copy-start(bf16[8,6,2,8224]{3,0,2,1:T(8,128)(2,1)} %copy.227) | copy-start | bytes 4737028
  559.1 9.5 %slice-start = ((s8[4792320]{0:T(1024)(128)(4,1)}), s8[4194304]{0:T(1024)(128)(4,1)S(1)}, s32[]{:S(2)}) async-start(s8[4792320]{0:T(1024)(128)(4,1)} %bitcast.117), calls=%async_computation.10 | async-start | bytes 8388608
  559.1 9.5 %slice-start.2 = ((s8[9584640]{0:T(1024)(128)(4,1)}), s8[4194304]{0:T(1024)(128)(4,1)S(1)}, s32[]{:S(2)}) async-start(s8[9584640]{0:T(1024)(128)(4,1)} %bitcast.120), calls=%async_computation.12 | async-start | bytes 8388608
  559.1 9.5 %slice-start.3 = ((s8[9584640]{0:T(1024)(128)(4,1)}), s8[4194304]{0:T(1024)(128)(4,1)S(1)}, s32[]{:S(2)}) async-start(s8[9584640]{0:T(1024)(128)(4,1)} %bitcast.120), calls=%async_computation.13 | async-start | bytes 8388608
  (9 other events, 43.1 us)
